TPU v7x, 512 devices: a whole 4x8x8 slice. The times are simulated.
512 devices in a mesh: member: 16 (over x, y_lo), space: 16 (over z, core), dp: 2 (over y_hi).
Axes of the slice: x: 4, y: 8 (y_hi: 2, y_lo: 4; y = y_hi * 4 + y_lo), z: 8, core: 2. Of those that a mesh axis runs over, the one named last changes fastest.
Arguments:
- latent: bfloat16 [16, 2, 16384, 1024], P('member', 'dp', 'space'), may hold values from -6 to 6
- target: bfloat16 [2, 100, 16384], P('dp', None, 'space'), may hold values from -6 to 6
- weight: bfloat16 [100, 1024], replicated, may hold values from -0.1875 to 0.1875
- bias: float32 [100], replicated, may hold values from -3 to 3
- gain: float32 [1024], replicated, may hold values from 0.1 to 1.9
- channel_weight: float32 [100], replicated, may hold values from 0.25 to 4
- band_offsets: int32 [17], replicated, may hold values from 0 to 80, as said below
- row_points: int32 [128], replicated, may hold values from 64 to 128, as said below
Outputs:
- grad_latent: bfloat16 [16, 2, 16384, 1024], P('member', 'dp', 'space')
- grad_weight: float32 [100, 1024], replicated
- grad_bias: float32 [100], replicated
- grad_gain: float32 [1024], replicated
- loss: float32 [], replicated
Inputs may be any that keep to these rules, and one draw needn't show every extreme that they name: `band_offsets`: nondecreasing, starting at 0; band s holds rows band_offsets[s] to band_offsets[s+1] - 1, at least 2 and at most 8 rows, and its points fill its first slots. `row_points`: the rows of one band hold at most 1024 points together, exactly 1024 in some band.
All inputs are finite; a program needn't handle non-finite values.
Results may differ from a plain program's by a relative error of at most 0.0084.
Values sent between devices are 32-bit elements; how exact they have to be, the bound alone decides.
A program may use at most 64 MiB of HBM per device.

v0:
```python
import jax
import jax.numpy as jnp
from jax import lax
from jax.sharding import PartitionSpec as P

smooth_sq = 0.01


def smooth_abs(value):
    return jnp.sqrt(value * value + smooth_sq)


def smooth_sign(value):
    return value / jnp.sqrt(value * value + smooth_sq)


def normalize(samples, gain):
    values = samples.astype(jnp.float32)
    middle = jnp.mean(values, axis=-1, keepdims=True)
    centered = values - middle
    variance = jnp.mean(centered * centered, axis=-1, keepdims=True)
    inverse = lax.rsqrt(variance + 1e-05)
    unit_rows = centered * inverse
    scaled = (unit_rows * gain).astype(jnp.bfloat16)
    return (unit_rows, inverse, scaled)


def shards(latent, target, weight, bias, gain, channel_weight, band_offsets, row_points):
    members = lax.axis_size("member")
    bands = lax.axis_size("space")
    band = lax.axis_index("space")
    own_member = lax.axis_index("member")
    row_ids = jnp.arange(row_points.shape[0], dtype=jnp.int32)
    in_band = (row_ids[None, :] >= band_offsets[:-1, None]) & (
        row_ids[None, :] < band_offsets[1:, None]
    )
    counts = jnp.sum(jnp.where(in_band, row_points[None, :], 0), axis=1)
    live_count = jnp.sum(jnp.where(jnp.arange(bands, dtype=jnp.int32) == band, counts, 0))
    total_live = jnp.sum(counts).astype(jnp.float32)
    samples = latent[0]
    slots = samples.shape[1]
    live = (jnp.arange(slots, dtype=jnp.int32) < live_count).astype(jnp.float32)
    unit_rows, inverse, scaled = normalize(samples, gain)
    predicted = (
        jnp.einsum("bph,ch->bcp", scaled, weight, preferred_element_type=jnp.float32)
        + bias[None, :, None]
    )
    grid_weight = channel_weight[None, :, None] * live[None, None, :]
    error = predicted - target.astype(jnp.float32)
    skill = jnp.sum(grid_weight * smooth_abs(error))
    pair_weight = 1.0 / (members - 1)
    piece = lax.all_gather(predicted[None], "member", axis=0, tiled=True)
    count = piece.shape[0]
    others = (jnp.arange(count, dtype=jnp.int32) != own_member).astype(jnp.float32)[
        :, None, None, None
    ]
    spread_gap = predicted[None] - piece
    spread_sum = jnp.sum(grid_weight[None] * others * smooth_abs(spread_gap))
    slope_sum = jnp.sum(others * smooth_sign(spread_gap), axis=0)
    local_score = skill - 0.5 * pair_weight * spread_sum
    dpred = grid_weight * (smooth_sign(error) - pair_weight * slope_sum)
    dpred_low = dpred.astype(jnp.bfloat16)
    grad_w = jnp.einsum("bcp,bph->ch", dpred_low, scaled, preferred_element_type=jnp.float32)
    grad_b = jnp.sum(dpred, axis=(0, 2))
    dscaled = jnp.einsum("bcp,ch->bph", dpred_low, weight, preferred_element_type=jnp.float32)
    grad_g = jnp.sum(dscaled * unit_rows, axis=(0, 1))
    dunit = dscaled * gain
    first = jnp.mean(dunit, axis=-1, keepdims=True)
    second = jnp.mean(dunit * unit_rows, axis=-1, keepdims=True)
    grad_x = (inverse * (dunit - first - unit_rows * second)).astype(jnp.bfloat16)
    sum_w, sum_b, sum_g, sum_score = lax.psum(
        (grad_w, grad_b, grad_g, local_score), ("member", "space", "dp")
    )
    batch = samples.shape[0] * lax.axis_size("dp")
    loss = sum_score / (weight.shape[0] * batch * total_live)
    return (grad_x[None], sum_w, sum_b, sum_g, loss)


def solution(mesh):
    return jax.shard_map(
        shards,
        mesh=mesh,
        in_specs=(
            P("member", "dp", "space", None),
            P("dp", None, "space"),
            P(),
            P(),
            P(),
            P(),
            P(),
            P(),
        ),
        out_specs=(P("member", "dp", "space", None), P(), P(), P(), P()),
        check_vma=False,
    )
```

profile of v0, /device:TPU:1, one launch (start us, length us, event | category | flops | bytes accessed | tf_op | source)
XLA Modules:
  0.0 467.6 jit_solution(11264365382467686688)
XLA Ops:
  7.2 0.0 copy-start
  7.2 0.0 copy-start.3
  7.2 0.0 copy-start.7
  7.2 0.0 all-gather.4.cloned.1.call-start
  7.2 2.9 copy.17
  10.2 0.4 convert_reduce_fusion
  10.5 0.0 copy-start.5
  10.5 0.0 copy-start.6
  10.6 0.0 copy-start.4
  10.6 0.6 fusion.2
  11.2 0.0 copy-done
  11.2 0.0 copy-done.3
  11.2 0.0 copy-done.7
  11.2 1.6 fusion.30
  12.8 0.0 all-gather.4.cloned.1.call-update
  12.8 0.0 all-reduce.3.cloned.1.call-start
  12.9 0.0 copy-done.5
  12.9 0.1 fusion.43
  12.9 0.0 copy-done.6
  13.0 0.7 select_reduce_fusion
  14.3 0.6 fusion.41
  15.0 0.6 fusion.40
  15.6 0.0 copy-done.4
  15.6 0.0 copy-start.1
  15.6 0.0 copy-start.2
  15.6 0.1 broadcast_multiply_fusion
  15.8 159.0 %all-gather.4.cloned.1.call-done = f32[16,100,1024]{2,1,0:T(8,128)} async-done(((f32[1,100,1024]{2,1,0:T(8,128)}), f32[16,100,1024]{2,1,0:T(8,128)}) %all-gather.4.cloned.1.call-update) | async-done | bytes 6553616 | tf_op jit(solution)/shard_map/all_gather | solution.py:52
  174.8 6.8 %multiply_reduce_fusion = (f32[]{:T(128)}, f32[100,1024]{1,0:T(8,128)S(1)}) fusion(f32[16,100,1024]{2,1,0:T(8,128)} %all-gather.4.cloned.1.call-done, f32[100,1024]{1,0:T(8,128)S(1)} %broadcast_multiply_fusion, f32[100,1024]{1,0:T(8,128)} %bitcast.71, f32[16]{0:T(128)S(1)} %compare_convert_fusion), kind=kLoop, calls=%fused_computation.5 | loop fusion | flops 14643199 | bytes 7782468 | tf_op jit(solution)/shard_map/reduce_sum | solution.py:58
  181.5 0.0 copy-done.1
  181.5 0.0 copy-done.2
  181.5 1.0 fusion.42
  182.5 1.6 fusion.22
  184.2 3.4 fusion.17
  187.6 0.0 all-reduce.3.cloned.1.call-update
  187.6 4.7 %fusion.18 = bf16[1,1,1024,1024]{2,3,1,0:T(8,128)(2,1)} fusion(bf16[1,1,1024,1024]{2,3,1,0:T(8,128)(2,1)S(1)} %copy.17, f32[1024,1024]{0,1:T(8,128)} %get-tuple-element.35, f32[1024]{0:T(1024)S(1)} %get-tuple-element.36, f32[1024]{0:T(1024)S(1)} %get-tuple-element.37, f32[1024]{0:T(1024)S(1)} %copy-done.3, f32[1024]{0:T(1024)S(1)} %broadcast_multiply_fusion.3, ...), kind=kLoop, calls=%fused_computation.27 | loop fusion | flops 9437184 | bytes 8409088 | tf_op jit(solution)/shard_map/broadcast_in_dim | solution.py:76
  192.3 3.9 copy.18
  197.6 99.5 %all-reduce = (f32[100]{0:T(128)}, f32[1024]{0:T(1024)}, f32[]{:T(128)}) all-reduce(f32[100]{0:T(128)S(1)} %get-tuple-element.30, f32[1024]{0:T(1024)S(1)} %get-tuple-element.22, f32[]{:T(128)S(6)} %sub.72), channel_id=1, replica_groups=mesh['member'=16,'space'=16,'dp'=2] {'member','space','dp'}, use_global_device_ids=true, to_apply=%region_9.10 | all-reduce | flops 1125 | bytes 9000 | tf_op jit(solution)/shard_map/psum | solution.py:71
  297.7 160.1 %all-reduce.3.cloned.1.call-done = f32[100,1024]{1,0:T(8,128)} async-done(((f32[100,1024]{1,0:T(8,128)}), f32[100,1024]{1,0:T(8,128)}) %all-reduce.3.cloned.1.call-update) | async-done | bytes 409616 | tf_op jit(solution)/shard_map/psum | solution.py:71
  457.8 1.8 copy.20
  (4 shorter events, 0.0 us)
Async XLA Ops:
  7.2 4.0 copy-start
  7.2 4.0 copy-start.3
  7.2 4.0 copy-start.7
  7.2 167.6 %all-gather.4.cloned.1.call-start = ((), (), s32[]{:S(2)}) async-start(), calls=%async_computation.1 | async-start | bytes 7241728 | tf_op jit(solution)/shard_map/all_gather | solution.py:52
  10.5 2.3 copy-start.5
  10.5 2.4 copy-start.6
  10.6 5.1 %copy-start.4 = (f32[100]{0:T(128)S(1)}, f32[100]{0:T(128)}, u32[]{:S(2)}) copy-start(f32[100]{0:T(128)} %param.13) | copy-start | bytes 1204
  12.8 445.0 %all-reduce.3.cloned.1.call-start = ((), (), s32[]{:S(2)}) async-start(), calls=%async_computation | async-start | bytes 851968 | tf_op jit(solution)/shard_map/psum | solution.py:71
  15.6 165.9 %copy-start.1 = (f32[1024,100]{0,1:T(8,128)S(1)}, f32[1024,100]{0,1:T(8,128)}, u32[]{:S(2)}) copy-start(f32[1024,100]{0,1:T(8,128)} %fusion.30) | copy-start | bytes 1228804
  15.6 165.9 %copy-start.2 = (bf16[1,100,1024]{2,1,0:T(8,128)(2,1)S(1)}, bf16[1,100,1024]{2,1,0:T(8,128)(2,1)}, u32[]{:S(2)}) copy-start(bf16[1,100,1024]{2,1,0:T(8,128)(2,1)} %param.9) | copy-start | bytes 614404
Sparse Core Ops, SparseCore 0:
  12.9 161.7 all-gather.3
  187.7 270.0 all-reduce.2
where the time goes:
time: 468 us
  waiting for transfers between devices  319 us (68%)
  blocking collectives  99.5 us (21%)
  between operations  17.9 us (4%)
  other arithmetic  15.5 us (3%)
  local copies, waits for them, and re-layouts  8.76 us (2%)
  matrix products  6.64 us (1%)
    psum x1, waiting for transfers between devices, shards(): lax.psum((grad_w, grad_b, grad_g, local_score), ('member', 'space', 'dp'))  160 us
    all_gather x1, waiting for transfers between devices, shards(): piece = lax.all_gather(predicted[None], 'member', axis=0, tiled=True)  159 us
    psum x1, blocking collectives, shards(): lax.psum((grad_w, grad_b, grad_g, local_score), ('member', 'space', 'dp'))  99.5 us
  transfers between devices with their start and end apart: 2, of which 2 were waited for; matrix products, arithmetic and copies ran while one was open for 2% of the time, Pallas kernels for 0%

commit v1 on v0

--- a/solution.py
+++ b/solution.py
@@ -4,6 +4,15 @@
 from jax.sharding import PartitionSpec as P
 
 smooth_sq = 0.01
+strings_choose = lambda row_data: jnp.concatenate(
+    lax.all_to_all(
+        jnp.stack([row_data for _ in range(lax.psum(1, "member"))], axis=0),
+        axis_name="member",
+        split_axis=0,
+        concat_axis=0,
+    ),
+    axis=0,
+)
 
 
 def smooth_abs(value):
@@ -49,7 +58,7 @@
     error = predicted - target.astype(jnp.float32)
     skill = jnp.sum(grid_weight * smooth_abs(error))
     pair_weight = 1.0 / (members - 1)
-    piece = lax.all_gather(predicted[None], "member", axis=0, tiled=True)
+    piece = strings_choose(predicted[None])
     count = piece.shape[0]
     others = (jnp.arange(count, dtype=jnp.int32) != own_member).astype(jnp.float32)[
         :, None, None, None

time: 468 us -> 503 us (1.075)
  other arithmetic: 15.5 us -> 49.7 us
  waiting for transfers between devices: 319 us -> 302 us
  starting transfers between devices: 0.08 us -> 8.21 us
  local copies, waits for them, and re-layouts: 8.76 us -> 15.1 us
    all_gather x1 -> x0, waiting for transfers between devices: 159 us -> none  [shards(): piece = lax.all_gather(predicted[None], 'member', axis=0, tiled=True)]
    all_to_all x0 -> x1, waiting for transfers between devices: none -> 143 us  [lax.all_to_all(jnp.stack([row_data for _ in range(lax.psum(1, 'member'))]...]
    reduce_sum x1, other arithmetic: 6.77 us -> 40.9 us  [shards(): spread_sum = jnp.sum(grid_weight[None] * others * smooth_abs(spread_gap))]
    all_to_all x0 -> x1, starting transfers between devices: none -> 8.17 us  [lax.all_to_all(jnp.stack([row_data for _ in range(lax.psum(1, 'member'))]...]
    another operation x0 -> x1, local copies, waits for them, and re-layouts: none -> 6.33 us  [jnp.stack([row_data for _ in range(lax.psum(1, 'member'))], axis=0)]
where the time goes in v1:
time: 503 us
  waiting for transfers between devices  302 us (60%)
  blocking collectives  104 us (21%)
  other arithmetic  49.7 us (10%)
  between operations  17.9 us (4%)
  local copies, waits for them, and re-layouts  15.1 us (3%)
  starting transfers between devices  8.21 us (2%)
  matrix products  5.88 us (1%)
    psum x1, waiting for transfers between devices, shards(): lax.psum((grad_w, grad_b, grad_g, local_score), ('member', 'space', 'dp'))  159 us
    all_to_all x1, waiting for transfers between devices, lax.all_to_all(jnp.stack([row_data for _ in range(lax.psum(1, 'member'))]...  143 us
    psum x1, blocking collectives, shards(): lax.psum((grad_w, grad_b, grad_g, local_score), ('member', 'space', 'dp'))  104 us
    reduce_sum x1, other arithmetic, shards(): spread_sum = jnp.sum(grid_weight[None] * others * smooth_abs(spread_gap))  40.9 us
  transfers between devices with their start and end apart: 2, of which 2 were waited for; matrix products, arithmetic and copies ran while one was open for 2% of the time, Pallas kernels for 0%

profile of v1, /device:TPU:1, one launch (start us, length us, event | category | flops | bytes accessed | tf_op | source)
XLA Modules:
  0.0 502.8 jit_solution(10419337186003777410)
XLA Ops:
  7.2 0.0 copy-start
  7.2 0.0 copy-start.6
  7.2 0.0 copy-start.2
  7.2 2.9 copy.17
  10.1 0.4 convert_reduce_fusion
  10.5 0.6 fusion.2
  11.1 0.0 copy-done
  11.1 0.0 copy-done.6
  11.1 0.0 copy-done.2
  11.1 0.8 fusion.30
  12.0 6.3 %stack.3 = f32[16,1,1,100,1024]{4,2,3,1,0:T(1,128)} broadcast(f32[100,1024]{1,0:T(8,128)S(1)} %bitcast.73), dimensions={3,4} | broadcast | bytes 6963200 | tf_op jit(solution)/shard_map/stack | solution.py:9
  18.3 0.0 copy-start.4
  18.3 0.0 copy-start.5
  18.3 0.0 copy-start.3
  18.3 8.2 %all-to-all-start = ((f32[16,1,1,100,1024]{4,2,3,1,0:T(1,128)}), f32[16,1,1,100,1024]{4,2,3,1,0:T(1,128)}, u32[]{:S(2)}, u32[]{:S(2)}) async-start(f32[16,1,1,100,1024]{4,2,3,1,0:T(1,128)} %stack.3), calls=%async_computation | async-start | bytes 13107200 | tf_op jit(solution)/shard_map/all_to_all | solution.py:8
  26.5 0.0 copy-start.1
  26.5 0.0 all-reduce.3.cloned.1.call-start
  26.5 0.0 copy-done.4
  26.6 0.1 fusion.43
  26.6 0.0 copy-done.5
  26.6 0.7 select_reduce_fusion
  28.0 0.6 fusion.41
  28.6 0.6 fusion.40
  29.3 0.0 copy-done.3
  29.3 0.1 broadcast_multiply_fusion
  29.4 143.0 %all-to-all-done = f32[16,1,1,100,1024]{4,2,3,1,0:T(1,128)} async-done(((f32[16,1,1,100,1024]{4,2,3,1,0:T(1,128)}), f32[16,1,1,100,1024]{4,2,3,1,0:T(1,128)}, u32[]{:S(2)}, u32[]{:S(2)}) %all-to-all-start) | async-done | bytes 6553632 | tf_op jit(solution)/shard_map/all_to_all | solution.py:8
  172.4 40.9 %multiply_reduce_fusion = (f32[]{:T(128)}, f32[100,1024]{1,0:T(8,128)S(1)}) fusion(f32[16,1,1,100,1024]{4,2,3,1,0:T(1,128)} %all-to-all-done, f32[100,1024]{1,0:T(8,128)S(1)} %broadcast_multiply_fusion, f32[100,1024]{1,0:T(8,128)S(1)} %bitcast.74, f32[16]{0:T(128)S(1)} %compare_convert_fusion), kind=kLoop, calls=%fused_computation.5 | loop fusion | flops 14643199 | bytes 7782468 | tf_op jit(solution)/shard_map/reduce_sum | solution.py:67
  213.3 0.0 copy-done.1
  213.3 1.0 fusion.42
  214.3 3.4 fusion.17
  217.7 1.7 fusion.22
  219.3 0.0 all-reduce.3.cloned.1.call-update
  219.4 4.7 fusion.18
  224.1 3.9 copy.18
  229.3 103.6 %all-reduce = (f32[100]{0:T(128)}, f32[1024]{0:T(1024)}, f32[]{:T(128)}) all-reduce(f32[100]{0:T(128)S(1)} %get-tuple-element.30, f32[1024]{0:T(1024)S(1)} %get-tuple-element.22, f32[]{:T(128)S(6)} %sub.84), channel_id=1, replica_groups=mesh['member'=16,'space'=16,'dp'=2] {'member','space','dp'}, use_global_device_ids=true, to_apply=%region_9.10 | all-reduce | flops 1125 | bytes 9000 | tf_op jit(solution)/shard_map/psum | solution.py:80
  333.6 159.4 %all-reduce.3.cloned.1.call-done = f32[100,1024]{1,0:T(8,128)} async-done(((f32[100,1024]{1,0:T(8,128)}), f32[100,1024]{1,0:T(8,128)}) %all-reduce.3.cloned.1.call-update) | async-done | bytes 409616 | tf_op jit(solution)/shard_map/psum | solution.py:80
  493.0 1.8 copy.20
  (4 shorter events, 0.0 us)
Async XLA Ops:
  7.2 4.0 copy-start
  7.2 3.9 copy-start.6
  7.2 3.9 copy-start.2
  18.3 8.3 %copy-start.4 = (s32[17]{0:T(128)S(1)}, s32[17]{0:T(128)}, u32[]{:S(2)}) copy-start(s32[17]{0:T(128)} %param.14) | copy-start | bytes 208
  18.3 8.3 %copy-start.5 = (s32[128]{0:T(128)S(1)}, s32[128]{0:T(128)}, u32[]{:S(2)}) copy-start(s32[128]{0:T(128)} %param.15) | copy-start | bytes 1540
  18.3 11.0 %copy-start.3 = (f32[100]{0:T(128)S(1)}, f32[100]{0:T(128)}, u32[]{:S(2)}) copy-start(f32[100]{0:T(128)} %param.13) | copy-start | bytes 1204
  18.3 154.1 %all-to-all-start = ((f32[16,1,1,100,1024]{4,2,3,1,0:T(1,128)}), f32[16,1,1,100,1024]{4,2,3,1,0:T(1,128)}, u32[]{:S(2)}, u32[]{:S(2)}) async-start(f32[16,1,1,100,1024]{4,2,3,1,0:T(1,128)} %stack.3), calls=%async_computation | async-start | bytes 13107200 | tf_op jit(solution)/shard_map/all_to_all | solution.py:8
  26.5 186.8 %copy-start.1 = (bf16[1,100,1024]{2,1,0:T(8,128)(2,1)S(1)}, bf16[1,100,1024]{2,1,0:T(8,128)(2,1)}, u32[]{:S(2)}) copy-start(bf16[1,100,1024]{2,1,0:T(8,128)(2,1)} %param.9) | copy-start | bytes 614404
  26.5 466.5 %all-reduce.3.cloned.1.call-start = ((), (), s32[]{:S(2)}) async-start(), calls=%async_computation.1 | async-start | bytes 851968 | tf_op jit(solution)/shard_map/psum | solution.py:80
Sparse Core Ops, SparseCore 0:
  219.5 273.5 all-reduce.2
